TPU v7x, 32 devices: a whole 2x2x4 slice. The times are simulated.
32 devices in a mesh: pair: 8 (over z, y), aux: 4 (over x, core).
Axes of the slice: x: 2, y: 2, z: 4, core: 2. Of those that a mesh axis runs over, the one named last changes fastest.
Arguments:
- amplitudes: float32 [896, 8, 896], P('aux', 'pair'), may hold values from -6 to 6
- fitting: float32 [4, 896, 896], P('aux', 'pair'), may hold values from -0.09375 to 0.09375
Outputs:
- ladder: float32 [896, 8, 896], P('aux', 'pair')
All inputs are finite; a program needn't handle non-finite values.
Results may differ from a plain program's by a relative error of at most 0.0001.
Values sent between devices are 32-bit elements; how exact they have to be, the bound alone decides.
A program may use at most 64 MiB of HBM per device.

v0:
```python
import jax
import jax.numpy as jnp
from jax import lax
from jax.sharding import PartitionSpec as P


def per_device(amplitudes, fitting):
    width = amplitudes.shape[2]
    pair_dev = amplitudes.shape[1]
    count_fit = fitting.shape[0]
    whole_fit = lax.all_gather(fitting, "pair", axis=1, tiled=True)
    whole_amp = lax.all_gather(amplitudes, "aux", axis=0, tiled=True)
    halves = jnp.einsum(
        "rpd,lbd->lrpb",
        whole_amp,
        whole_fit,
        precision=lax.Precision.HIGHEST,
        preferred_element_type=jnp.float32,
    )
    halves = halves.reshape(count_fit, width, pair_dev * width)
    result = lax.psum_scatter(
        jnp.einsum(
            "lac,lcx->ax",
            whole_fit,
            halves,
            precision=lax.Precision.HIGHEST,
            preferred_element_type=jnp.float32,
        ),
        "aux",
        scatter_dimension=0,
        tiled=True,
    )
    return result.reshape(result.shape[0], pair_dev, width)


def solution(mesh):
    in_specs = (P("aux", "pair", None), P("aux", "pair", None))
    out_specs = P("aux", "pair", None)
    return jax.shard_map(
        per_device, mesh=mesh, in_specs=in_specs, out_specs=out_specs, check_vma=False
    )
```

profile of v0, /device:TPU:0, one launch (start us, length us, event | category | flops | bytes accessed | tf_op | source)
XLA Modules:
  0.0 180.0 jit_solution(6608431639948401352)
XLA Ops:
  6.5 0.0 all-gather.5.cloned.1.call-start
  6.5 0.7 all-gather.5.cloned.1.call-update
  7.3 0.0 all-gather.3.cloned.1.call-start
  7.3 0.7 all-gather.3.cloned.1.call-update
  8.0 0.0 reduce-scatter.4.cloned.1.call-start
  8.1 32.5 %all-gather.5.cloned.1.call-done = f32[896,1,896]{2,1,0:T(1,128)} async-done(((f32[224,1,896]{2,1,0:T(1,128)}), f32[896,1,896]{2,1,0:T(1,128)}) %all-gather.5.cloned.1.call-update) | async-done | bytes 3211280 | tf_op jit(solution)/shard_map/all_gather | solution.py:12
  40.5 62.9 %all-gather.3.cloned.1.call-done = f32[1,896,896]{2,1,0:T(8,128)} async-done(((f32[1,112,896]{2,1,0:T(8,128)}), f32[1,896,896]{2,1,0:T(8,128)}) %all-gather.3.cloned.1.call-update) | async-done | bytes 3211280 | tf_op jit(solution)/shard_map/all_gather | solution.py:11
  103.4 0.0 copy-start
  103.4 14.9 %fusion = f32[896,896]{1,0:T(8,128)S(1)} fusion(f32[896,1,896]{2,1,0:T(1,128)} %all-gather.5.cloned.1.call-done, f32[1,896,896]{2,1,0:T(8,128)} %all-gather.3.cloned.1.call-done), kind=kOutput, calls=%fused_computation | convolution fusion | flops 8631877632 | bytes 9633792 | tf_op jit(solution)/shard_map/rpd,lbd->lrpb/dot_general | solution.py:13
  118.3 0.0 copy-done
  118.3 11.7 %fusion.7 = f32[896,896]{0,1:T(8,128)S(1)} fusion(f32[1,896,896]{2,1,0:T(8,128)S(1)} %copy-done, f32[896,896]{1,0:T(8,128)S(1)} %fusion), kind=kOutput, calls=%fused_computation.7 | convolution fusion | flops 8631877632 | bytes 9633792 | tf_op jit(solution)/shard_map/lac,lcx->ax/dot_general | solution.py:22
  129.9 3.0 %copy.5 = f32[896,896]{1,0:T(8,128)} copy(f32[896,896]{0,1:T(8,128)S(1)} %fusion.7) | data formatting | bytes 6422528
  133.0 0.0 reduce-scatter.4.cloned.1.call-update
  133.0 37.1 %reduce-scatter.4.cloned.1.call-done = f32[224,896]{1,0:T(8,128)} async-done(((f32[896,896]{1,0:T(8,128)}), f32[224,896]{1,0:T(8,128)}) %reduce-scatter.4.cloned.1.call-update) | async-done | bytes 802832
  170.1 1.4 copy.6
  171.5 1.9 %copy.4 = f32[224,1,896]{2,1,0:T(1,128)} copy(f32[224,1,896]{0,2,1:T(8,128)S(1)} %bitcast.23) | data formatting | bytes 1605632 | tf_op jit(solution)/shard_map/reshape | solution.py:33
Async XLA Ops:
  6.5 34.0 %all-gather.5.cloned.1.call-start = ((), (), s32[]{:S(2)}) async-start(), calls=%async_computation.2 | async-start | bytes 4014080 | tf_op jit(solution)/shard_map/all_gather | solution.py:12
  7.3 96.2 %all-gather.3.cloned.1.call-start = ((), (), s32[]{:S(2)}) async-start(), calls=%async_computation.1 | async-start | bytes 3612672 | tf_op jit(solution)/shard_map/all_gather | solution.py:11
  8.0 162.1 %reduce-scatter.4.cloned.1.call-start = ((), (), s32[]{:S(2)}) async-start(), calls=%async_computation.3 | async-start | bytes 4014080
  103.4 14.9 %copy-start = (f32[1,896,896]{2,1,0:T(8,128)S(1)}, f32[1,896,896]{2,1,0:T(8,128)}, u32[]{:S(2)}) copy-start(f32[1,896,896]{2,1,0:T(8,128)} %all-gather.3.cloned.1.call-done) | copy-start | bytes 9633796
Sparse Core Ops, SparseCore 0:
  8.9 31.5 all-gather.4
  42.7 60.6 all-gather.2
  133.1 36.9 reduce-scatter.3
where the time goes:
time: 180 us
  waiting for transfers between devices  134 us (74%)
  matrix products  26.5 us (15%)
  between operations  13.1 us (7%)
  local copies, waits for them, and re-layouts  6.39 us (4%)
    all_gather x1, waiting for transfers between devices, per_device(): whole_fit = lax.all_gather(fitting, 'pair', axis=1, tiled=True)  62.9 us
    unnamed x4, waiting for transfers between devices  38.5 us
    all_gather x1, waiting for transfers between devices, per_device(): whole_amp = lax.all_gather(amplitudes, 'aux', axis=0, tiled=True)  32.5 us
    dot_general x1, matrix products, per_device(): jnp.einsum('rpd,lbd->lrpb', whole_amp, whole_fit, precision=lax.Precision...  14.9 us
    dot_general x1, matrix products, per_device(): jnp.einsum('lac,lcx->ax', whole_fit, halves, precision=lax.Precision.HIGH...  11.7 us
    unnamed x4, local copies, waits for them, and re-layouts  4.45 us
  transfers between devices with their start and end apart: 3, of which 3 were waited for; matrix products, arithmetic and copies ran while one was open for 0% of the time, Pallas kernels for 0%

commit v1 on v0

--- a/solution.py
+++ b/solution.py
@@ -9,7 +9,9 @@
     pair_dev = amplitudes.shape[1]
     count_fit = fitting.shape[0]
     whole_fit = lax.all_gather(fitting, "pair", axis=1, tiled=True)
-    whole_amp = lax.all_gather(amplitudes, "aux", axis=0, tiled=True)
+    whole_amp = jnp.concatenate(
+        lax.all_to_all(jnp.stack([amplitudes] * lax.axis_size("aux")), "aux", 0, 0), axis=0
+    )
     halves = jnp.einsum(
         "rpd,lbd->lrpb",
         whole_amp,

time: 180 us -> 149 us (0.83)
  waiting for transfers between devices: 134 us -> 58.8 us
  blocking collectives: 0 us -> 41.6 us
  local copies, waits for them, and re-layouts: 6.39 us -> 9.43 us
    all_gather x1, waiting for transfers between devices: 62.9 us -> 20.9 us  [per_device(): whole_fit = lax.all_gather(fitting, 'pair', axis=1, tiled=True)]
    all_to_all x0 -> x1, blocking collectives: none -> 41.6 us  [per_device(): lax.all_to_all(jnp.stack([amplitudes] * lax.axis_size('aux')), 'aux', 0, 0)]
    all_gather x1 -> x0, waiting for transfers between devices: 32.5 us -> none  [per_device(): whole_amp = lax.all_gather(amplitudes, 'aux', axis=0, tiled=True)]
    unnamed x4 -> x6, local copies, waits for them, and re-layouts: 4.45 us -> 5.83 us
    unnamed x4 -> x3, waiting for transfers between devices: 38.5 us -> 37.9 us
  transfers between devices with their start and end apart: 3 -> 2, of which waited for: 3 -> 2; matrix products, arithmetic and copies ran while one was open for 0% -> 2% of each run, Pallas kernels for 0% -> 0%
where the time goes in v1:
time: 149 us
  waiting for transfers between devices  58.8 us (39%)
  blocking collectives  41.6 us (28%)
  matrix products  25.5 us (17%)
  between operations  13.4 us (9%)
  local copies, waits for them, and re-layouts  9.43 us (6%)
    all_to_all x1, blocking collectives, per_device(): lax.all_to_all(jnp.stack([amplitudes] * lax.axis_size('aux')), 'aux', 0, 0)  41.6 us
    unnamed x3, waiting for transfers between devices  37.9 us
    all_gather x1, waiting for transfers between devices, per_device(): whole_fit = lax.all_gather(fitting, 'pair', axis=1, tiled=True)  20.9 us
    dot_general x1, matrix products, per_device(): jnp.einsum('rpd,lbd->lrpb', whole_amp, whole_fit, precision=lax.Precision...  14 us
    dot_general x1, matrix products, per_device(): jnp.einsum('lac,lcx->ax', whole_fit, halves, precision=lax.Precision.HIGH...  11.5 us
    unnamed x6, local copies, waits for them, and re-layouts  5.83 us
  transfers between devices with their start and end apart: 2, of which 2 were waited for; matrix products, arithmetic and copies ran while one was open for 2% of the time, Pallas kernels for 0%

profile of v1, /device:TPU:0, one launch (start us, length us, event | category | flops | bytes accessed | tf_op | source)
XLA Modules:
  0.0 148.8 jit_solution(8494522418118383180)
XLA Ops:
  6.5 0.0 all-gather.2.cloned.1.call-start
  6.5 0.7 all-gather.2.cloned.1.call-update
  7.3 0.0 reduce-scatter.4.cloned.1.call-start
  7.3 1.2 copy.10
  8.5 1.7 %stack.2 = f32[4,224,1,896]{3,2,1,0:T(1,128)S(1)} broadcast(f32[224,896]{1,0:T(8,128)S(1)} %bitcast.27), dimensions={1,3} | broadcast | bytes 4014080 | tf_op jit(solution)/shard_map/stack | solution.py:13
  10.2 41.6 %all_to_all.5 = f32[4,224,1,896]{3,2,1,0:T(1,128)S(1)} all-to-all(f32[4,224,1,896]{3,2,1,0:T(1,128)S(1)} %stack.2), channel_id=1, replica_groups=mesh['pair'=8,'aux'=4] {'aux'}, dimensions={0} | all-to-all | bytes 6422528 | tf_op jit(solution)/shard_map/all_to_all | solution.py:13
  51.8 0.2 copy.8
  52.0 20.9 %all-gather.2.cloned.1.call-done = f32[1,896,896]{2,1,0:T(8,128)} async-done(((f32[1,112,896]{2,1,0:T(8,128)}), f32[1,896,896]{2,1,0:T(8,128)}) %all-gather.2.cloned.1.call-update) | async-done | bytes 3211280 | tf_op jit(solution)/shard_map/all_gather | solution.py:11
  72.9 0.0 copy-start
  72.9 14.0 %fusion.3 = f32[896,896]{1,0:T(8,128)S(1)} fusion(f32[896,896]{1,0:T(8,128)S(1)} %bitcast.25, f32[1,896,896]{2,1,0:T(8,128)} %all-gather.2.cloned.1.call-done), kind=kOutput, calls=%fused_computation.3 | convolution fusion | flops 8631877632 | bytes 9633792 | tf_op jit(solution)/shard_map/rpd,lbd->lrpb/dot_general | solution.py:15
  87.0 0.0 copy-done
  87.0 11.5 %fusion.5 = f32[896,896]{0,1:T(8,128)S(1)} fusion(f32[1,896,896]{2,1,0:T(8,128)S(1)} %copy-done, f32[896,896]{1,0:T(8,128)S(1)} %fusion.3), kind=kOutput, calls=%fused_computation.5 | convolution fusion | flops 8631877632 | bytes 9633792 | tf_op jit(solution)/shard_map/lac,lcx->ax/dot_general | solution.py:24
  98.4 3.0 %copy.5 = f32[896,896]{1,0:T(8,128)} copy(f32[896,896]{0,1:T(8,128)S(1)} %fusion.5) | data formatting | bytes 6422528
  101.4 0.0 reduce-scatter.4.cloned.1.call-update
  101.5 37.1 %reduce-scatter.4.cloned.1.call-done = f32[224,896]{1,0:T(8,128)} async-done(((f32[896,896]{1,0:T(8,128)}), f32[224,896]{1,0:T(8,128)}) %reduce-scatter.4.cloned.1.call-update) | async-done | bytes 802832
  138.6 1.4 copy.6
  140.0 1.9 %copy.4 = f32[224,1,896]{2,1,0:T(1,128)} copy(f32[224,1,896]{0,2,1:T(8,128)S(1)} %bitcast.26) | data formatting | bytes 1605632 | tf_op jit(solution)/shard_map/reshape | solution.py:35
Async XLA Ops:
  6.5 66.4 %all-gather.2.cloned.1.call-start = ((), (), s32[]{:S(2)}) async-start(), calls=%async_computation.2 | async-start | bytes 3612672 | tf_op jit(solution)/shard_map/all_gather | solution.py:11
  7.3 131.3 %reduce-scatter.4.cloned.1.call-start = ((), (), s32[]{:S(2)}) async-start(), calls=%async_computation.3 | async-start | bytes 4014080
  72.9 14.0 %copy-start = (f32[1,896,896]{2,1,0:T(8,128)S(1)}, f32[1,896,896]{2,1,0:T(8,128)}, u32[]{:S(2)}) copy-start(f32[1,896,896]{2,1,0:T(8,128)} %all-gather.2.cloned.1.call-done) | copy-start | bytes 9633796
Sparse Core Ops, SparseCore 0:
  9.5 63.3 all-gather.1
  101.6 36.9 reduce-scatter.3
